TPU v7x, 32 devices: a whole 2x2x4 slice. The times are simulated.
32 devices in a mesh: det: 8 (over y, x, core), row: 4 (over z).
Axes of the slice: x: 2, y: 2, z: 4, core: 2. Of those that a mesh axis runs over, the one named last changes fastest.
Arguments:
- coefficients: bfloat16 [8, 2048, 200], P('det', 'row'), may hold values from -1 to 1
- amplitudes: bfloat16 [8], P('det'), may hold values from -3 to 3
- plan: int32 [8, 2, 1], P('det'), may hold values 0 or 1
Outputs:
- density: float32 [2048, 2048], P('det', 'row')
All inputs are finite; a program needn't handle non-finite values. No bound on the sum of `plan` on one device may be relied on, other than what follows from the above.
Results may differ from a plain program's by a relative error of at most 0.0024.
Values may be sent and summed in bfloat16 or wider, within the bound.
A program may use at most 64 MiB of HBM per device.

v0:
```python
import jax
import jax.numpy as jnp
from jax import lax
from jax.sharding import PartitionSpec as P

ORDER = 2


def shifted(block, axis, distance):
    devices = range(lax.axis_size(axis))
    route = [((i - distance) % len(devices), i) for i in devices]
    return lax.ppermute(block, axis, route)


def neumann(correlation):
    identity = jnp.eye(correlation.shape[-1], dtype=jnp.float32)
    remainder = identity - correlation
    inverse = identity + jnp.zeros_like(correlation)
    for level in range(ORDER):
        inverse = identity + jnp.einsum(
            "...ab,...bc->...ac", remainder, inverse, precision=lax.Precision.HIGHEST
        )
    return inverse


def on_device(coefficients, amplitudes, plan):
    masks = plan.astype(jnp.float32)
    ket_amps = amplitudes.astype(jnp.float32)
    distances = plan.shape[1]
    ket_whole = lax.all_gather(coefficients, "row", axis=1, tiled=True)
    accum = jnp.zeros(
        (coefficients.shape[0], coefficients.shape[2], coefficients.shape[1]), jnp.float32
    )
    visitor = (coefficients, amplitudes)
    for step in range(distances):
        if step > 0:
            visitor = shifted((visitor[0], visitor[1]), "det", 1)
        visitor_full = lax.all_gather(visitor[0], "row", axis=1, tiled=True)
        correlation = jnp.einsum(
            "ina,jnb->ijab", visitor_full, ket_whole, preferred_element_type=jnp.float32
        )
        weight = visitor[1].astype(jnp.float32)[:, None] * ket_amps[None, :] * masks[:, step, :].T
        scaled = (weight[:, :, None, None] * neumann(correlation)).astype(jnp.bfloat16)
        accum = accum + jnp.einsum(
            "ijba,ina->jbn", scaled, visitor[0], preferred_element_type=jnp.float32
        )
    folded = accum.astype(jnp.bfloat16)
    return lax.psum_scatter(
        jnp.einsum("jmb,jbn->mn", ket_whole, folded, preferred_element_type=jnp.float32),
        "det",
        scatter_dimension=0,
        tiled=True,
    )


def solution(mesh):
    placed = (P("det", "row", None), P("det"), P("det", None, None))
    return jax.shard_map(
        on_device, mesh=mesh, in_specs=placed, out_specs=P("det", "row"), check_vma=False
    )
```

profile of v0, /device:TPU:0, one launch (start us, length us, event | category | flops | bytes accessed | tf_op | source)
XLA Modules:
  0.0 117.4 jit_solution(16775029854525567413)
XLA Ops:
  6.5 0.0 reduce-scatter.2.cloned.1.call-start
  6.5 0.5 collective-permute-start
  7.0 2.6 %collective-permute-start.1 = (bf16[1,512,200]{1,2,0:T(8,128)(2,1)}, bf16[1,512,200]{1,2,0:T(8,128)(2,1)S(1)}, u32[]{:S(2)}, u32[]{:S(2)}) collective-permute-start(bf16[1,512,200]{1,2,0:T(8,128)(2,1)} %param.3), channel_id=1, source_target_pairs={{28,0},{0,4},{4,8},{8,12},{12,16},{16,20},{20,24},{24,28},{29,1},{... | collective-permute-start | bytes 614408 | tf_op jit(solution)/shard_map/ppermute | solution.py:12
  10.3 20.4 %all_gather.7 = bf16[1,2048,200]{1,2,0:T(8,128)(2,1)S(1)} all-gather(bf16[1,512,200]{1,2,0:T(8,128)(2,1)} %param.3), channel_id=1, replica_groups=mesh['det'=8,'row'=4] {'row'}, dimensions={1}, use_global_device_ids=true | all-gather | bytes 1024000 | tf_op jit(solution)/shard_map/all_gather | solution.py:30
  30.7 0.7 convert_element_type.44
  31.3 0.6 fusion.17
  31.9 0.4 fusion.4
  32.4 0.4 convolution_add_fusion.4
  33.3 0.6 fusion.7
  33.9 1.1 fusion.15
  35.0 0.0 collective-permute-done
  36.3 0.0 collective-permute-done.1
  36.3 18.2 %all_gather.8 = bf16[1,2048,200]{1,2,0:T(8,128)(2,1)S(1)} all-gather(bf16[1,512,200]{1,2,0:T(8,128)(2,1)S(1)} %collective-permute-done.1), channel_id=1, replica_groups=mesh['det'=8,'row'=4] {'row'}, dimensions={1}, use_global_device_ids=true | all-gather | bytes 1024000 | tf_op jit(solution)/shard_map/all_gather | solution.py:38
  54.5 0.4 fusion.6
  55.0 0.4 convolution_add_fusion.3
  55.3 0.6 fusion.8
  55.9 2.9 %convolution_bitcast_fusion = f32[2048,512]{0,1:T(8,128)} fusion(f32[200,512]{1,0:T(8,128)S(1)} %fusion.15, bf16[200,200]{1,0:T(8,128)(2,1)S(1)} %fusion.8, bf16[1,2048,200]{1,2,0:T(8,128)(2,1)S(1)} %all_gather.7, bf16[1,512,200]{1,2,0:T(8,128)(2,1)S(1)} %collective-permute-done.1), kind=kOutput, calls=%fused_computation | convolution fusion | flops 460595200 | bytes 5707904 | tf_op jit(solution)/shard_map/jmb,jbn->mn/dot_general | solution.py:49
  58.8 0.0 reduce-scatter.2.cloned.1.call-update
  58.8 49.7 %reduce-scatter.2.cloned.1.call-done = f32[256,512]{0,1:T(8,128)} async-done(((f32[2048,512]{0,1:T(8,128)}), f32[256,512]{0,1:T(8,128)}) %reduce-scatter.2.cloned.1.call-update) | async-done | bytes 524304 | tf_op jit(solution)/shard_map/reduce_scatter | solution.py:48
  108.6 2.0 %copy.4 = f32[256,512]{1,0:T(8,128)} copy(f32[256,512]{0,1:T(8,128)} %reduce-scatter.2.cloned.1.call-done) | data formatting | bytes 1048576 | tf_op jit(solution)/shard_map/reduce_scatter | solution.py:48
Async XLA Ops:
  6.5 102.0 %reduce-scatter.2.cloned.1.call-start = ((), (), s32[]{:S(2)}) async-start(), calls=%async_computation.1 | async-start | bytes 4718592 | tf_op jit(solution)/shard_map/reduce_scatter | solution.py:48
  6.5 28.5 %collective-permute-start = (bf16[1]{0:T(256)(128)(2,1)}, bf16[1]{0:T(256)(128)(2,1)}, u32[]{:S(2)}, u32[]{:S(2)}) collective-permute-start(bf16[1]{0:T(256)(128)(2,1)} %param.4), channel_id=1, source_target_pairs={{28,0},{0,4},{4,8},{8,12},{12,16},{16,20},{20,24},{24,28},{29,1},{... | collective-permute-start | bytes 14 | tf_op jit(solution)/shard_map/ppermute | solution.py:12
  7.0 29.2 %collective-permute-start.1 = (bf16[1,512,200]{1,2,0:T(8,128)(2,1)}, bf16[1,512,200]{1,2,0:T(8,128)(2,1)S(1)}, u32[]{:S(2)}, u32[]{:S(2)}) collective-permute-start(bf16[1,512,200]{1,2,0:T(8,128)(2,1)} %param.3), channel_id=1, source_target_pairs={{28,0},{0,4},{4,8},{8,12},{12,16},{16,20},{20,24},{24,28},{29,1},{... | collective-permute-start | bytes 614408 | tf_op jit(solution)/shard_map/ppermute | solution.py:12
Sparse Core Ops, SparseCore 0:
  59.0 49.5 reduce-scatter.1
where the time goes:
time: 118 us; the launch traced here: 117 us
  waiting for transfers between devices  49.7 us (42%)
  blocking collectives  38.6 us (33%)
  between operations  15.9 us (13%)
  matrix products  6.78 us (6%)
  starting transfers between devices  3.08 us (3%)
  local copies, waits for them, and re-layouts  2.63 us (2%)
    reduce_scatter x1, waiting for transfers between devices, on_device(): lax.psum_scatter(jnp.einsum('jmb,jbn->mn', ket_whole, folded, preferred_e...  49.7 us
    all_gather x1, blocking collectives, on_device(): ket_whole = lax.all_gather(coefficients, 'row', axis=1, tiled=True)  20.4 us
    all_gather x1, blocking collectives, on_device(): visitor_full = lax.all_gather(visitor[0], 'row', axis=1, tiled=True)  18.2 us
    ppermute x2, starting transfers between devices, shifted(): return lax.ppermute(block, axis, route)  3.08 us
    dot_general x1, matrix products, on_device(): jnp.einsum('jmb,jbn->mn', ket_whole, folded, preferred_element_type=jnp.f...  2.88 us
  transfers between devices with their start and end apart: 3, of which 1 were waited for; matrix products, arithmetic and copies ran while one was open for 3% of the time, Pallas kernels for 0%

commit v1 on v0

--- a/solution.py
+++ b/solution.py
@@ -4,6 +4,22 @@
 from jax.sharding import PartitionSpec as P
 
 ORDER = 2
+
+
+def ring_product(x, axis, dim, term):
+    size, index, extent = (lax.axis_size(axis), lax.axis_index(axis), x.shape[dim])
+    right = [(i, (i + 1) % size) for i in range(size)]
+    downward = [(i, (i - 1) % size) for i in range(size)]
+    half = size // 2
+    from_left = from_right = x
+    running = term(x, index * extent)
+    for step in range(1, half + 1):
+        from_left = lax.ppermute(from_left, axis, right)
+        if step < size - half:
+            from_right = lax.ppermute(from_right, axis, downward)
+            running = running + term(from_right, (index + step) % size * extent)
+        running = running + term(from_left, (index - step) % size * extent)
+    return running
 
 
 def shifted(block, axis, distance):
@@ -35,9 +51,16 @@
     for step in range(distances):
         if step > 0:
             visitor = shifted((visitor[0], visitor[1]), "det", 1)
-        visitor_full = lax.all_gather(visitor[0], "row", axis=1, tiled=True)
-        correlation = jnp.einsum(
-            "ina,jnb->ijab", visitor_full, ket_whole, preferred_element_type=jnp.float32
+        correlation = ring_product(
+            visitor[0],
+            "row",
+            1,
+            lambda part, offset: jnp.einsum(
+                "ina,jnb->ijab",
+                part,
+                lax.dynamic_slice_in_dim(ket_whole, offset, part.shape[1], axis=1),
+                preferred_element_type=jnp.float32,
+            ),
         )
         weight = visitor[1].astype(jnp.float32)[:, None] * ket_amps[None, :] * masks[:, step, :].T
         scaled = (weight[:, :, None, None] * neumann(correlation)).astype(jnp.bfloat16)

time: 118 us -> 127 us (1.076)
  waiting for transfers between devices: 49.7 us -> 66.7 us
  blocking collectives: 38.6 us -> 22.7 us
  starting transfers between devices: 3.08 us -> 10.6 us
    all_gather x1 -> x0, blocking collectives: 18.2 us -> none  [on_device(): visitor_full = lax.all_gather(visitor[0], 'row', axis=1, tiled=True)]
    ppermute x0 -> x6, waiting for transfers between devices: none -> 18.1 us  [the longest x4 18.1 us: ring_product(): from_left = lax.ppermute(from_left, axis, right)]
    ppermute x0 -> x6, starting transfers between devices: none -> 9.01 us  [the longest x2 8.89 us: ring_product(): from_right = lax.ppermute(from_right, axis, downward)]
    all_gather x1, blocking collectives: 20.4 us -> 22.7 us  [on_device(): ket_whole = lax.all_gather(coefficients, 'row', axis=1, tiled=True)]
    dot_general x2 -> x8, matrix products: 0.84 us -> 2.82 us  [on_device(): jnp.einsum('ina,jnb->ijab', part, lax.dynamic_slice_in_dim(ket_whole, off...]
    ppermute x2, starting transfers between devices: 3.08 us -> 1.61 us  [shifted(): return lax.ppermute(block, axis, route)]
  transfers between devices with their start and end apart: 3 -> 9, of which waited for: 1 -> 3; matrix products, arithmetic and copies ran while one was open for 3% -> 4% of each run, Pallas kernels for 0% -> 0%
where the time goes in v1:
time: 127 us
  waiting for transfers between devices  66.7 us (53%)
  blocking collectives  22.7 us (18%)
  between operations  16.1 us (13%)
  starting transfers between devices  10.6 us (8%)
  matrix products  7.83 us (6%)
  local copies, waits for them, and re-layouts  2.65 us (2%)
    reduce_scatter x1, waiting for transfers between devices, on_device(): lax.psum_scatter(jnp.einsum('jmb,jbn->mn', ket_whole, folded, preferred_e...  48.5 us
    all_gather x1, blocking collectives, on_device(): ket_whole = lax.all_gather(coefficients, 'row', axis=1, tiled=True)  22.7 us
    ppermute x4, waiting for transfers between devices, ring_product(): from_left = lax.ppermute(from_left, axis, right)  18.1 us
    ppermute x2, starting transfers between devices, ring_product(): from_right = lax.ppermute(from_right, axis, downward)  8.89 us
    dot_general x1, matrix products, on_device(): jnp.einsum('jmb,jbn->mn', ket_whole, folded, preferred_element_type=jnp.f...  2.89 us
    dot_general x8, matrix products, on_device(): jnp.einsum('ina,jnb->ijab', part, lax.dynamic_slice_in_dim(ket_whole, off...  2.82 us
  transfers between devices with their start and end apart: 9, of which 3 were waited for; matrix products, arithmetic and copies ran while one was open for 4% of the time, Pallas kernels for 0%

profile of v1, /device:TPU:0, one launch (start us, length us, event | category | flops | bytes accessed | tf_op | source)
XLA Modules:
  0.0 127.2 jit_solution(13889590285134708576)
XLA Ops:
  6.5 0.0 copy-start
  6.5 0.0 reduce-scatter.2.cloned.1.call-start
  6.5 5.1 %collective-permute-start = (bf16[1,512,200]{1,2,0:T(8,128)(2,1)}, bf16[1,512,200]{1,2,0:T(8,128)(2,1)S(1)}, u32[]{:S(2)}, u32[]{:S(2)}) collective-permute-start(bf16[1,512,200]{1,2,0:T(8,128)(2,1)} %param.3), channel_id=1, source_target_pairs={{0,3},{1,0},{2,1},{3,2},{4,7},{5,4},{6,5},{7,6},{8,11},{9,8},{10,9... | collective-permute-start | bytes 614408 | tf_op jit(solution)/shard_map/ppermute | solution.py:19
  11.6 0.0 collective-permute-start.4
  11.6 0.0 collective-permute-start.1
  11.6 1.6 %collective-permute-start.3 = (bf16[1]{0:T(256)(128)(2,1)}, bf16[1]{0:T(256)(128)(2,1)}, u32[]{:S(2)}, u32[]{:S(2)}) collective-permute-start(bf16[1]{0:T(256)(128)(2,1)} %param.4), channel_id=1, source_target_pairs={{28,0},{0,4},{4,8},{8,12},{12,16},{16,20},{20,24},{24,28},{29,1},{... | collective-permute-start | bytes 14 | tf_op jit(solution)/shard_map/ppermute | solution.py:28
  13.9 22.7 %all_gather.3 = bf16[1,2048,200]{1,2,0:T(8,128)(2,1)S(1)} all-gather(bf16[1,512,200]{1,2,0:T(8,128)(2,1)} %param.3), channel_id=1, replica_groups=mesh['det'=8,'row'=4] {'row'}, dimensions={1}, use_global_device_ids=true | all-gather | bytes 1024000 | tf_op jit(solution)/shard_map/all_gather | solution.py:46
  36.6 0.7 convert_element_type.44
  37.2 0.6 fusion.50
  38.5 1.2 fusion.30
  39.6 0.0 collective-permute-done.3
  40.9 0.0 collective-permute-done.4
  40.9 0.1 collective-permute-start.6
  41.0 3.8 %collective-permute-start.5 = (bf16[1,512,200]{1,2,0:T(8,128)(2,1)S(1)}, bf16[1,512,200]{1,2,0:T(8,128)(2,1)S(1)}, u32[]{:S(2)}, u32[]{:S(2)}) collective-permute-start(bf16[1,512,200]{1,2,0:T(8,128)(2,1)S(1)} %collective-permute-done.4), channel_id=1, source_target_pairs={{0,3},{1,0},{2,1},{3,2},{4,7},{5,4},{6,5},{7,6},{8,11},{9,8},{10,9... | collective-permute-start | bytes 614408 | tf_op jit(solution)/shard_map/ppermute | solution.py:19
  44.8 0.0 collective-permute-done.1
  44.8 0.0 collective-permute-start.2
  44.8 0.0 collective-permute-done
  44.8 0.2 convolution_add_fusion.8
  45.1 0.2 convolution_add_fusion.7
  45.3 0.2 fusion.17
  45.5 11.3 %collective-permute-done.2 = bf16[1,512,200]{1,2,0:T(8,128)(2,1)S(1)} collective-permute-done((bf16[1,512,200]{1,2,0:T(8,128)(2,1)S(1)}, bf16[1,512,200]{1,2,0:T(8,128)(2,1)S(1)}, u32[]{:S(2)}, u32[]{:S(2)}) %collective-permute-start.2) | collective-permute-done | bytes 204832 | tf_op jit(solution)/shard_map/ppermute | solution.py:17
  56.8 0.2 fusion.6
  57.1 0.4 convolution_add_fusion.10
  57.4 0.6 fusion.9
  58.0 0.0 collective-permute-done.6
  58.0 0.1 collective-permute-start.7
  58.1 0.0 copy-done
  58.1 0.2 fusion.28
  58.3 0.0 collective-permute-done.5
  58.3 0.2 convolution_add_fusion.4
  58.6 0.2 convolution_add_fusion.3
  58.8 6.8 %collective-permute-done.7 = bf16[1,512,200]{1,2,0:T(8,128)(2,1)S(1)} collective-permute-done((bf16[1,512,200]{1,2,0:T(8,128)(2,1)S(1)}, bf16[1,512,200]{1,2,0:T(8,128)(2,1)S(1)}, u32[]{:S(2)}, u32[]{:S(2)}) %collective-permute-start.7) | collective-permute-done | bytes 204832 | tf_op jit(solution)/shard_map/ppermute | solution.py:17
  65.6 0.2 fusion.8
  65.9 0.4 convolution_add_fusion.9
  66.2 0.6 fusion.10
  66.8 2.9 %convolution_bitcast_fusion = f32[2048,512]{0,1:T(8,128)} fusion(f32[200,512]{1,0:T(8,128)S(1)} %fusion.28, bf16[200,200]{1,0:T(8,128)(2,1)S(1)} %fusion.10, bf16[1,2048,200]{1,2,0:T(8,128)(2,1)S(1)} %all_gather.3, bf16[1,512,200]{1,2,0:T(8,128)(2,1)S(1)} %collective-permute-done.4), kind=kOutput, calls=%fused_computation | convolution fusion | flops 460595200 | bytes 5707904 | tf_op jit(solution)/shard_map/jmb,jbn->mn/dot_general | solution.py:72
  69.7 0.0 reduce-scatter.2.cloned.1.call-update
  69.8 48.5 %reduce-scatter.2.cloned.1.call-done = f32[256,512]{0,1:T(8,128)} async-done(((f32[2048,512]{0,1:T(8,128)}), f32[256,512]{0,1:T(8,128)}) %reduce-scatter.2.cloned.1.call-update) | async-done | bytes 524304 | tf_op jit(solution)/shard_map/reduce_scatter | solution.py:71
  118.3 2.0 %copy.4 = f32[256,512]{1,0:T(8,128)} copy(f32[256,512]{0,1:T(8,128)} %reduce-scatter.2.cloned.1.call-done) | data formatting | bytes 1048576 | tf_op jit(solution)/shard_map/reduce_scatter | solution.py:71
Async XLA Ops:
  6.5 51.6 %copy-start = (bf16[1,512,200]{1,2,0:T(8,128)(2,1)S(1)}, bf16[1,512,200]{1,2,0:T(8,128)(2,1)}, u32[]{:S(2)}) copy-start(bf16[1,512,200]{1,2,0:T(8,128)(2,1)} %param.3) | copy-start | bytes 614404
  6.5 111.7 %reduce-scatter.2.cloned.1.call-start = ((), (), s32[]{:S(2)}) async-start(), calls=%async_computation.1 | async-start | bytes 4718592 | tf_op jit(solution)/shard_map/reduce_scatter | solution.py:71
  6.5 38.3 %collective-permute-start = (bf16[1,512,200]{1,2,0:T(8,128)(2,1)}, bf16[1,512,200]{1,2,0:T(8,128)(2,1)S(1)}, u32[]{:S(2)}, u32[]{:S(2)}) collective-permute-start(bf16[1,512,200]{1,2,0:T(8,128)(2,1)} %param.3), channel_id=1, source_target_pairs={{0,3},{1,0},{2,1},{3,2},{4,7},{5,4},{6,5},{7,6},{8,11},{9,8},{10,9... | collective-permute-start | bytes 614408 | tf_op jit(solution)/shard_map/ppermute | solution.py:19
  11.6 29.3 %collective-permute-start.4 = (bf16[1,512,200]{1,2,0:T(8,128)(2,1)}, bf16[1,512,200]{1,2,0:T(8,128)(2,1)S(1)}, u32[]{:S(2)}, u32[]{:S(2)}) collective-permute-start(bf16[1,512,200]{1,2,0:T(8,128)(2,1)} %param.3), channel_id=1, source_target_pairs={{28,0},{0,4},{4,8},{8,12},{12,16},{16,20},{20,24},{24,28},{29,1},{... | collective-permute-start | bytes 614408 | tf_op jit(solution)/shard_map/ppermute | solution.py:28
  11.6 33.2 %collective-permute-start.1 = (bf16[1,512,200]{1,2,0:T(8,128)(2,1)}, bf16[1,512,200]{1,2,0:T(8,128)(2,1)S(1)}, u32[]{:S(2)}, u32[]{:S(2)}) collective-permute-start(bf16[1,512,200]{1,2,0:T(8,128)(2,1)} %param.3), channel_id=1, source_target_pairs={{0,1},{1,2},{2,3},{3,0},{4,5},{5,6},{6,7},{7,4},{8,9},{9,10},{10,1... | collective-permute-start | bytes 614408 | tf_op jit(solution)/shard_map/ppermute | solution.py:17
  11.6 28.0 %collective-permute-start.3 = (bf16[1]{0:T(256)(128)(2,1)}, bf16[1]{0:T(256)(128)(2,1)}, u32[]{:S(2)}, u32[]{:S(2)}) collective-permute-start(bf16[1]{0:T(256)(128)(2,1)} %param.4), channel_id=1, source_target_pairs={{28,0},{0,4},{4,8},{8,12},{12,16},{16,20},{20,24},{24,28},{29,1},{... | collective-permute-start | bytes 14 | tf_op jit(solution)/shard_map/ppermute | solution.py:28
  40.9 17.1 %collective-permute-start.6 = (bf16[1,512,200]{1,2,0:T(8,128)(2,1)S(1)}, bf16[1,512,200]{1,2,0:T(8,128)(2,1)S(1)}, u32[]{:S(2)}, u32[]{:S(2)}) collective-permute-start(bf16[1,512,200]{1,2,0:T(8,128)(2,1)S(1)} %collective-permute-done.4), channel_id=1, source_target_pairs={{0,1},{1,2},{2,3},{3,0},{4,5},{5,6},{6,7},{7,4},{8,9},{9,10},{10,1... | collective-permute-start | bytes 614408 | tf_op jit(solution)/shard_map/ppermute | solution.py:17
  41.0 17.3 %collective-permute-start.5 = (bf16[1,512,200]{1,2,0:T(8,128)(2,1)S(1)}, bf16[1,512,200]{1,2,0:T(8,128)(2,1)S(1)}, u32[]{:S(2)}, u32[]{:S(2)}) collective-permute-start(bf16[1,512,200]{1,2,0:T(8,128)(2,1)S(1)} %collective-permute-done.4), channel_id=1, source_target_pairs={{0,3},{1,0},{2,1},{3,2},{4,7},{5,4},{6,5},{7,6},{8,11},{9,8},{10,9... | collective-permute-start | bytes 614408 | tf_op jit(solution)/shard_map/ppermute | solution.py:19
  44.8 12.0 %collective-permute-start.2 = (bf16[1,512,200]{1,2,0:T(8,128)(2,1)S(1)}, bf16[1,512,200]{1,2,0:T(8,128)(2,1)S(1)}, u32[]{:S(2)}, u32[]{:S(2)}) collective-permute-start(bf16[1,512,200]{1,2,0:T(8,128)(2,1)S(1)} %collective-permute-done.1), channel_id=1, source_target_pairs={{0,1},{1,2},{2,3},{3,0},{4,5},{5,6},{6,7},{7,4},{8,9},{9,10},{10,1... | collective-permute-start | bytes 614408 | tf_op jit(solution)/shard_map/ppermute | solution.py:17
  58.0 7.6 %collective-permute-start.7 = (bf16[1,512,200]{1,2,0:T(8,128)(2,1)S(1)}, bf16[1,512,200]{1,2,0:T(8,128)(2,1)S(1)}, u32[]{:S(2)}, u32[]{:S(2)}) collective-permute-start(bf16[1,512,200]{1,2,0:T(8,128)(2,1)S(1)} %collective-permute-done.6), channel_id=1, source_target_pairs={{0,1},{1,2},{2,3},{3,0},{4,5},{5,6},{6,7},{7,4},{8,9},{9,10},{10,1... | collective-permute-start | bytes 614408 | tf_op jit(solution)/shard_map/ppermute | solution.py:17
Sparse Core Ops, SparseCore 0:
  69.9 48.3 reduce-scatter.1

commit v2 on v0

--- a/solution.py
+++ b/solution.py
@@ -35,7 +35,7 @@
     for step in range(distances):
         if step > 0:
             visitor = shifted((visitor[0], visitor[1]), "det", 1)
-        visitor_full = lax.all_gather(visitor[0], "row", axis=1, tiled=True)
+        visitor_full = jnp.concatenate(lax.all_gather(visitor[0], "row"), axis=1)
         correlation = jnp.einsum(
             "ina,jnb->ijab", visitor_full, ket_whole, preferred_element_type=jnp.float32
         )

time: 118 us -> 134 us (1.14)
  blocking collectives: 38.6 us -> 56.5 us
    all_gather x1 -> x2, blocking collectives: 18.2 us -> 36.1 us  [on_device(): visitor_full = jnp.concatenate(lax.all_gather(visitor[0], 'row'), axis=1)]
  transfers between devices with their start and end apart: 3 -> 3, of which waited for: 1 -> 1; matrix products, arithmetic and copies ran while one was open for 3% -> 2% of each run, Pallas kernels for 0% -> 0%
where the time goes in v2:
time: 134 us
  blocking collectives  56.5 us (42%)
  waiting for transfers between devices  49.3 us (37%)
  between operations  16 us (12%)
  matrix products  5.89 us (4%)
  starting transfers between devices  3.08 us (2%)
  local copies, waits for them, and re-layouts  2.81 us (2%)
    reduce_scatter x1, waiting for transfers between devices, on_device(): lax.psum_scatter(jnp.einsum('jmb,jbn->mn', ket_whole, folded, preferred_e...  49.2 us
    all_gather x2, blocking collectives, on_device(): visitor_full = jnp.concatenate(lax.all_gather(visitor[0], 'row'), axis=1)  36.1 us
    all_gather x1, blocking collectives, on_device(): ket_whole = lax.all_gather(coefficients, 'row', axis=1, tiled=True)  20.4 us
    ppermute x2, starting transfers between devices, shifted(): return lax.ppermute(block, axis, route)  3.08 us
    dot_general x1, matrix products, on_device(): jnp.einsum('jmb,jbn->mn', ket_whole, folded, preferred_element_type=jnp.f...  2.88 us
  transfers between devices with their start and end apart: 3, of which 1 were waited for; matrix products, arithmetic and copies ran while one was open for 2% of the time, Pallas kernels for 0%

profile of v2, /device:TPU:0, one launch (start us, length us, event | category | flops | bytes accessed | tf_op | source)
XLA Modules:
  0.0 134.2 jit_solution(2136398914960074546)
XLA Ops:
  6.5 0.0 copy-start
  6.5 0.0 reduce-scatter.2.cloned.1.call-start
  6.5 0.5 collective-permute-start
  7.0 2.6 %collective-permute-start.1 = (bf16[1,512,200]{1,2,0:T(8,128)(2,1)}, bf16[1,512,200]{1,2,0:T(8,128)(2,1)S(1)}, u32[]{:S(2)}, u32[]{:S(2)}) collective-permute-start(bf16[1,512,200]{1,2,0:T(8,128)(2,1)} %param.3), channel_id=1, source_target_pairs={{28,0},{0,4},{4,8},{8,12},{12,16},{16,20},{20,24},{24,28},{29,1},{... | collective-permute-start | bytes 614408 | tf_op jit(solution)/shard_map/ppermute | solution.py:12
  10.3 20.4 %all_gather.15 = bf16[1,2048,200]{1,2,0:T(8,128)(2,1)S(1)} all-gather(bf16[1,512,200]{1,2,0:T(8,128)(2,1)} %param.3), channel_id=1, replica_groups=mesh['det'=8,'row'=4] {'row'}, dimensions={1}, use_global_device_ids=true | all-gather | bytes 1024000 | tf_op jit(solution)/shard_map/all_gather | solution.py:30
  30.7 18.4 %all-gather = bf16[4,512,200]{1,2,0:T(8,128)(2,1)S(1)} all-gather(bf16[1,512,200]{1,2,0:T(8,128)(2,1)} %param.3), channel_id=2, replica_groups=mesh['det'=8,'row'=4] {'row'}, dimensions={0}, use_global_device_ids=true | all-gather | bytes 1024000 | tf_op jit(solution)/shard_map/all_gather | solution.py:38
  49.1 0.7 convert_element_type.44
  49.8 0.6 fusion.16
  50.4 0.1 copy.11
  50.5 0.4 fusion.4
  50.9 0.4 convolution_add_fusion.4
  52.0 0.6 fusion.7
  52.6 0.0 copy-done
  52.6 0.2 fusion.14
  52.8 0.0 collective-permute-done
  54.0 0.0 collective-permute-done.1
  54.0 17.7 %all-gather.1 = bf16[4,512,200]{1,2,0:T(8,128)(2,1)S(1)} all-gather(bf16[1,512,200]{1,2,0:T(8,128)(2,1)S(1)} %collective-permute-done.1), channel_id=3, replica_groups=mesh['det'=8,'row'=4] {'row'}, dimensions={0}, use_global_device_ids=true | all-gather | bytes 1024000 | tf_op jit(solution)/shard_map/all_gather | solution.py:38
  71.7 0.1 copy.12
  71.8 0.4 fusion.6
  72.2 0.4 convolution_add_fusion.3
  72.6 0.6 fusion.8
  73.2 2.9 %convolution_bitcast_fusion = f32[2048,512]{0,1:T(8,128)} fusion(f32[200,512]{1,0:T(8,128)S(1)} %fusion.14, bf16[200,200]{1,0:T(8,128)(2,1)S(1)} %fusion.8, bf16[1,2048,200]{1,2,0:T(8,128)(2,1)S(1)} %all_gather.15, bf16[1,512,200]{1,2,0:T(8,128)(2,1)S(1)} %collective-permute-done.1), kind=kOutput, calls=%fused_computation | convolution fusion | flops 460595200 | bytes 5707904 | tf_op jit(solution)/shard_map/jmb,jbn->mn/dot_general | solution.py:49
  76.1 0.0 reduce-scatter.2.cloned.1.call-update
  76.1 49.2 %reduce-scatter.2.cloned.1.call-done = f32[256,512]{0,1:T(8,128)} async-done(((f32[2048,512]{0,1:T(8,128)}), f32[256,512]{0,1:T(8,128)}) %reduce-scatter.2.cloned.1.call-update) | async-done | bytes 524304 | tf_op jit(solution)/shard_map/reduce_scatter | solution.py:48
  125.3 2.0 %copy.10 = f32[256,512]{1,0:T(8,128)} copy(f32[256,512]{0,1:T(8,128)} %reduce-scatter.2.cloned.1.call-done) | data formatting | bytes 1048576 | tf_op jit(solution)/shard_map/reduce_scatter | solution.py:48
Async XLA Ops:
  6.5 46.0 %copy-start = (bf16[1,512,200]{1,2,0:T(8,128)(2,1)S(1)}, bf16[1,512,200]{1,2,0:T(8,128)(2,1)}, u32[]{:S(2)}) copy-start(bf16[1,512,200]{1,2,0:T(8,128)(2,1)} %param.3) | copy-start | bytes 614404
  6.5 118.8 %reduce-scatter.2.cloned.1.call-start = ((), (), s32[]{:S(2)}) async-start(), calls=%async_computation.1 | async-start | bytes 4718592 | tf_op jit(solution)/shard_map/reduce_scatter | solution.py:48
  6.5 46.3 %collective-permute-start = (bf16[1]{0:T(256)(128)(2,1)}, bf16[1]{0:T(256)(128)(2,1)}, u32[]{:S(2)}, u32[]{:S(2)}) collective-permute-start(bf16[1]{0:T(256)(128)(2,1)} %param.4), channel_id=1, source_target_pairs={{28,0},{0,4},{4,8},{8,12},{12,16},{16,20},{20,24},{24,28},{29,1},{... | collective-permute-start | bytes 14 | tf_op jit(solution)/shard_map/ppermute | solution.py:12
  7.0 47.0 %collective-permute-start.1 = (bf16[1,512,200]{1,2,0:T(8,128)(2,1)}, bf16[1,512,200]{1,2,0:T(8,128)(2,1)S(1)}, u32[]{:S(2)}, u32[]{:S(2)}) collective-permute-start(bf16[1,512,200]{1,2,0:T(8,128)(2,1)} %param.3), channel_id=1, source_target_pairs={{28,0},{0,4},{4,8},{8,12},{12,16},{16,20},{20,24},{24,28},{29,1},{... | collective-permute-start | bytes 614408 | tf_op jit(solution)/shard_map/ppermute | solution.py:12
Sparse Core Ops, SparseCore 0:
  76.2 49.0 reduce-scatter.1
